TPU v7x, 512 devices: a whole 4x4x16 slice. The times are simulated.
512 devices in a mesh: branch: 8 (over y_lo, x), sky: 64 (over z, y_hi, core).
Axes of the slice: x: 4, y: 4 (y_hi: 2, y_lo: 2; y = y_hi * 2 + y_lo), z: 16, core: 2. Of those that a mesh axis runs over, the one named last changes fastest.
Arguments:
- sky_maps: bfloat16 [8, 64, 16384], P('branch', None, 'sky'), may hold values from -6 to 6
- footprint: int32 [8, 16384], P('branch', 'sky'), may hold values 0 or 1
- neighbours: int32 [9, 16384], P(None, 'sky'), may hold values from -1 to 16383, as said below
- enc_weight: bfloat16 [8, 6, 9, 64, 64], P('branch'), may hold values from -0.1875 to 0.1875
- join_weight: bfloat16 [256, 512], P(None, 'branch'), may hold values from -0.25 to 0.25
- dec_weight: bfloat16 [9, 256, 256], P(None, 'branch'), may hold values from -0.125 to 0.125
- cotangent: bfloat16 [256, 16384], P('branch', 'sky'), may hold values from -6 to 6
Outputs:
- map_grads: bfloat16 [8, 64, 16384], P('branch', None, 'sky')
- weight_grads: float32 [8, 6, 9, 64, 64], P('branch')
Inputs may be any that keep to these rules, and one draw needn't show every extreme that they name: `neighbours`: slot 4 of each row is the row itself; every other entry is -1 or a row index that differs from the row's own by at most 256.
All inputs are finite; a program needn't handle non-finite values. No bound on the sum of `footprint` on one device may be relied on, other than what follows from the above.
Results may differ from a plain program's by a relative error of at most 0.017.
Values may be sent and summed in bfloat16 or wider, within the bound.
No kernel may reach another device: no remote copies, remote signals or barrier semaphores. Data moves between devices by JAX's collectives and lax.ppermute only.
A program may use at most 64 MiB of HBM per device.

v0:
```python
import math
import jax
import jax.numpy as jnp
from jax import lax
from jax.sharding import PartitionSpec as P


def from_behind(value, axis, by):
    peers = lax.axis_size(axis)
    pairs = [(i, i + by) for i in range(peers) if 0 <= i + by < peers]
    return lax.ppermute(value, axis, pairs)


def with_halo(cells, sides, width):
    for axis, dim in sides:
        count = lax.axis_size(axis)
        ends = count - 1
        head = lax.slice_in_dim(cells, 0, width, axis=dim)
        tail = lax.slice_in_dim(cells, cells.shape[dim] - width, cells.shape[dim], axis=dim)
        cells = jnp.concatenate(
            [
                lax.ppermute(tail, axis, [(i, (i + 1) % count) for i in range(ends)]),
                cells,
                lax.ppermute(head, axis, [((i + 1) % count, i) for i in range(ends)]),
            ],
            axis=dim,
        )
    return cells


def silu_slope(value):
    sigmoid = jax.nn.sigmoid(value)
    return sigmoid * (1.0 + value * (1.0 - sigmoid))


def flat_taps(weight):
    return jnp.transpose(weight, (1, 2, 0)).reshape(weight.shape[1], -1)


def pick_columns(padded, position, present):
    channels = padded.shape[0]
    picked = jnp.take(padded, position.reshape(-1), axis=1).reshape(channels, 9, -1)
    return jnp.where(present[None], picked, jnp.zeros((), padded.dtype))


def spread_columns(contrib, position, present, channels, total_span):
    contrib = jnp.where(present[None], contrib.reshape(channels, 9, -1), 0.0)
    target = jnp.zeros((channels, total_span), jnp.float32)
    return target.at[:, position.reshape(-1)].add(contrib.reshape(channels, -1))


def fold_rims(padded, row_count):
    lower = from_behind(padded[:, :row_count].astype(jnp.bfloat16), "sky", -1).astype(jnp.float32)
    upper = from_behind(padded[:, 2 * row_count :].astype(jnp.bfloat16), "sky", 1).astype(
        jnp.float32
    )
    return padded[:, row_count : 2 * row_count] + lower + upper


def fold_unit_rims(padded, row_count):
    lower = from_behind(padded[:, :row_count].astype(jnp.bfloat16), "sky", -1).astype(jnp.float32)
    upper = from_behind(padded[:, 2 * row_count :].astype(jnp.bfloat16), "sky", 1).astype(
        jnp.float32
    )
    return padded[:, row_count : 2 * row_count] + lower + upper


def per_device(sky_maps, footprint, neighbours, enc_weight, join_weight, dec_weight, cotangent):
    row_count = sky_maps.shape[2]
    channels = sky_maps.shape[1]
    own_start = lax.axis_index("sky") * row_count
    first_row = own_start - row_count
    present = neighbours >= 0
    position = jnp.where(present, neighbours - first_row, 0)
    retained = footprint[0].astype(jnp.float32)[None, :]
    weights = enc_weight[0]
    depth = weights.shape[0]
    hidden = sky_maps[0]
    padded_list = []
    pre_list = []
    for layer_index in range(depth):
        padded = with_halo(hidden, (("sky", 1),), row_count)
        picked = pick_columns(padded, position, present)
        preact = jnp.dot(
            flat_taps(weights[layer_index]),
            picked.reshape(-1, row_count),
            preferred_element_type=jnp.float32,
        )
        hidden = (retained * (hidden.astype(jnp.float32) + jax.nn.silu(preact))).astype(
            jnp.bfloat16
        )
        padded_list.append(padded)
        pre_list.append(preact)
    partial_sum = jnp.dot(join_weight, hidden, preferred_element_type=jnp.float32)
    unit_share = lax.psum_scatter(
        partial_sum.astype(jnp.bfloat16), "branch", scatter_dimension=0, tiled=True
    ).astype(jnp.float32)
    slope_share = silu_slope(unit_share).astype(jnp.bfloat16)
    full_width = dec_weight.shape[2]
    dec_terms = lax.dot_general(
        flat_taps(dec_weight),
        cotangent,
        (((0,), (0,)), ((), ())),
        preferred_element_type=jnp.float32,
    )
    unit_pad = spread_columns(dec_terms, position, present, full_width, 3 * row_count)
    summed = lax.psum(fold_unit_rims(unit_pad, row_count), "branch")
    all_slopes = lax.all_gather(slope_share, "branch", axis=0, tiled=True)
    unit_grad = (summed * all_slopes.astype(jnp.float32)).astype(jnp.bfloat16)
    gradient = lax.dot_general(
        join_weight, unit_grad, (((0,), (0,)), ((), ())), preferred_element_type=jnp.float32
    )
    normalizer = 1.0 / math.sqrt(row_count * lax.axis_size("sky"))
    layer_grads = [None] * depth
    for layer_index in reversed(range(depth)):
        masked = retained * gradient
        act_grad = (masked * silu_slope(pre_list[layer_index])).astype(jnp.bfloat16)
        picked = pick_columns(padded_list[layer_index], position, present).reshape(-1, row_count)
        tap_grads = lax.dot_general(
            act_grad, picked, (((1,), (1,)), ((), ())), preferred_element_type=jnp.float32
        )
        layer_grads[layer_index] = jnp.transpose(
            tap_grads.reshape(channels, channels, 9), (2, 0, 1)
        )
        spread = lax.dot_general(
            flat_taps(weights[layer_index]),
            act_grad,
            (((0,), (0,)), ((), ())),
            preferred_element_type=jnp.float32,
        )
        gradient = masked + fold_rims(
            spread_columns(spread, position, present, channels, 3 * row_count), row_count
        )
    summed_weights = lax.psum(jnp.stack(layer_grads), "sky") * normalizer
    return (gradient.astype(jnp.bfloat16)[None], summed_weights[None])


def solution(mesh):
    in_specs = (
        P("branch", None, "sky"),
        P("branch", "sky"),
        P(None, "sky"),
        P("branch", None, None, None, None),
        P(None, "branch"),
        P(None, "branch", None),
        P("branch", "sky"),
    )
    out_specs = (P("branch", None, "sky"), P("branch", None, None, None, None))
    return jax.shard_map(
        per_device, mesh=mesh, in_specs=in_specs, out_specs=out_specs, check_vma=False
    )
```

profile of v0, /device:TPU:1, one launch (start us, length us, event | category | flops | bytes accessed | tf_op | source)
XLA Modules:
  0.0 955.9 jit_solution(9312221840940899464)
XLA Ops:
  7.2 6.2 collective-permute-start.2
  13.4 3.9 collective-permute-start.3
  21.3 4.7 gather_fusion
  34.3 3.1 collective-permute-done.5
  37.6 4.7 gather_fusion.1
  50.8 2.9 collective-permute-done.7
  53.8 4.7 gather_fusion.2
  65.2 5.2 collective-permute-done.9
  70.6 4.7 gather_fusion.3
  82.9 14.1 %scatter_custom_fusion = f32[256,768]{0,1:T(8,128)S(1)} fusion(s32[2304]{0:T(1024)S(1)} %fusion.94, f32[2304,256]{1,0:T(8,128)} %bitcast.220, f32[]{:T(128)} %constant.17.clone.1), kind=kCustom, calls=%fused_computation.80 | custom fusion | flops 589824 | bytes 786944 | tf_op jit(solution)/shard_map/scatter-add | solution.py:49
  98.0 4.7 gather_fusion.4
  105.9 5.8 collective-permute-start.12
  116.3 5.1 collective-permute-start.1
  121.6 4.7 gather_fusion.5
  133.1 48.7 %reduce-scatter.4.cloned.1.call-done = bf16[32,256]{1,0:T(8,128)(2,1)} async-done(((bf16[256,256]{1,0:T(8,128)(2,1)}), bf16[32,256]{1,0:T(8,128)(2,1)}) %reduce-scatter.4.cloned.1.call-update) | async-done | bytes 16400 | tf_op jit(solution)/shard_map/reduce_scatter | solution.py:95
  182.6 21.8 %all_gather.3 = bf16[256,256]{1,0:T(8,128)(2,1)S(1)} all-gather(bf16[32,256]{1,0:T(8,128)(2,1)S(1)} %fusion.83), channel_id=1, replica_groups=mesh['branch'=8,'sky'=64] {'branch'}, dimensions={0}, use_global_device_ids=true | all-gather | bytes 147456 | tf_op jit(solution)/shard_map/all_gather | solution.py:108
  204.5 69.8 %all-reduce.3.cloned.1.call-done = f32[256,256]{0,1:T(8,128)} async-done(((f32[256,256]{0,1:T(8,128)}), f32[256,256]{0,1:T(8,128)}) %all-reduce.3.cloned.1.call-update) | async-done | bytes 262160 | tf_op jit(solution)/shard_map/psum | solution.py:107
  276.8 16.2 %scatter_custom_fusion.1 = f32[64,768]{0,1:T(8,128)S(1)} fusion(s32[2304]{0:T(1024)} %copy-done.40, f32[64,2304]{0,1:T(8,128)S(1)} %copy.134, f32[]{:T(128)} %constant.17.clone.1, pred[2304]{0:T(1024)(128)(4,1)S(1)} %broadcast_in_dim.154), kind=kCustom, calls=%fused_computation.31 | custom fusion | flops 294912 | bytes 789760 | tf_op jit(solution)/shard_map/scatter-add | solution.py:49
  293.1 7.5 collective-permute-start.14
  300.6 4.2 collective-permute-start.15
  307.7 16.0 %scatter_custom_fusion.2 = f32[64,768]{0,1:T(8,128)S(1)} fusion(s32[2304]{0:T(1024)} %copy-done.40, f32[64,2304]{0,1:T(8,128)S(1)} %copy.138, f32[]{:T(128)} %constant.17.clone.1, pred[2304]{0:T(1024)(128)(4,1)S(1)} %broadcast_in_dim.154), kind=kCustom, calls=%fused_computation.29 | custom fusion | flops 294912 | bytes 789760 | tf_op jit(solution)/shard_map/scatter-add | solution.py:49
  325.9 5.9 collective-permute-start.17
  334.4 16.2 %scatter_custom_fusion.3 = f32[64,768]{0,1:T(8,128)S(1)} fusion(s32[2304]{0:T(1024)} %copy-done.40, f32[64,2304]{0,1:T(8,128)S(1)} %copy.142, f32[]{:T(128)} %constant.17.clone.1, pred[2304]{0:T(1024)(128)(4,1)S(1)} %broadcast_in_dim.154), kind=kCustom, calls=%fused_computation.27 | custom fusion | flops 294912 | bytes 789760 | tf_op jit(solution)/shard_map/scatter-add | solution.py:49
  352.6 5.3 collective-permute-start.19
  360.7 16.0 %scatter_custom_fusion.4 = f32[64,768]{0,1:T(8,128)S(1)} fusion(s32[2304]{0:T(1024)} %copy-done.40, f32[64,2304]{0,1:T(8,128)S(1)} %copy.146, f32[]{:T(128)} %constant.17.clone.1, pred[2304]{0:T(1024)(128)(4,1)S(1)} %broadcast_in_dim.154), kind=kCustom, calls=%fused_computation.25 | custom fusion | flops 294912 | bytes 789760 | tf_op jit(solution)/shard_map/scatter-add | solution.py:49
  378.9 5.7 collective-permute-start.21
  387.8 16.0 %scatter_custom_fusion.5 = f32[64,768]{0,1:T(8,128)S(1)} fusion(s32[2304]{0:T(1024)} %copy-done.40, f32[64,2304]{0,1:T(8,128)S(1)} %copy.150, f32[]{:T(128)} %constant.17.clone.1, pred[2304]{0:T(1024)(128)(4,1)S(1)} %broadcast_in_dim.154), kind=kCustom, calls=%fused_computation.23 | custom fusion | flops 294912 | bytes 789760 | tf_op jit(solution)/shard_map/scatter-add | solution.py:49
  406.0 5.6 collective-permute-start.23
  418.3 16.0 %scatter_custom_fusion.6 = f32[64,768]{0,1:T(8,128)S(1)} fusion(s32[2304]{0:T(1024)} %copy-done.40, f32[64,2304]{0,1:T(8,128)S(1)} %copy.154, f32[]{:T(128)} %constant.17.clone.1, pred[2304]{0:T(1024)(128)(4,1)S(1)} %broadcast_in_dim.154), kind=kCustom, calls=%fused_computation.21 | custom fusion | flops 294912 | bytes 789760 | tf_op jit(solution)/shard_map/scatter-add | solution.py:49
  436.4 5.7 collective-permute-start.25
  443.8 502.4 %all-reduce.5.cloned.1.call-done = f32[6,9,64,64]{3,2,1,0:T(8,128)} async-done(((f32[6,9,64,64]{3,2,1,0:T(8,128)}), f32[6,9,64,64]{3,2,1,0:T(8,128)}) %all-reduce.5.cloned.1.call-update) | async-done | bytes 884752 | tf_op jit(solution)/shard_map/psum | solution.py:134
  946.2 2.9 multiply_bitcast_fusion
  (240 shorter events, 84.1 us)
Async XLA Ops:
  7.2 121.8 %copy-start = (bf16[256,64]{0,1:T(8,128)(2,1)S(1)}, bf16[256,64]{0,1:T(8,128)(2,1)}, u32[]{:S(2)}) copy-start(bf16[256,64]{0,1:T(8,128)(2,1)} %param.13) | copy-start | bytes 98308
  7.2 174.7 %reduce-scatter.4.cloned.1.call-start = ((), (), s32[]{:S(2)}) async-start(), calls=%async_computation.3 | async-start | bytes 147456 | tf_op jit(solution)/shard_map/reduce_scatter | solution.py:95
  7.2 12.3 %collective-permute-start.2 = (bf16[64,256]{1,0:T(8,128)(2,1)}, bf16[64,256]{1,0:T(8,128)(2,1)S(1)}, u32[]{:S(2)}, u32[]{:S(2)}) collective-permute-start(bf16[64,256]{1,0:T(8,128)(2,1)} %bitcast.241), channel_id=1, source_target_pairs={{0,1},{1,2},{2,3},{3,4},{4,5},{5,6},{6,7},{7,8},{8,9},{9,10},{10,1... | collective-permute-start | bytes 98312 | tf_op jit(solution)/shard_map/ppermute | solution.py:22
  13.4 7.0 collective-permute-start.3
  28.4 5.9 collective-permute-start.4
  30.7 6.7 collective-permute-start.5
  44.6 6.2 collective-permute-start.6
  46.6 7.1 collective-permute-start.7
  60.8 4.4 collective-permute-start.8
  63.0 7.4 collective-permute-start.9
  78.5 19.3 %collective-permute-start.10 = (bf16[64,256]{1,0:T(8,128)(2,1)S(1)}, bf16[64,256]{1,0:T(8,128)(2,1)S(1)}, u32[]{:S(2)}, u32[]{:S(2)}) collective-permute-start(bf16[64,256]{1,0:T(8,128)(2,1)S(1)} %get-tuple-element.35), channel_id=1, source_target_pairs={{0,1},{1,2},{2,3},{3,4},{4,5},{5,6},{6,7},{7,8},{8,9},{9,10},{10,1... | collective-permute-start | bytes 98312 | tf_op jit(solution)/shard_map/ppermute | solution.py:22
  80.4 17.4 %collective-permute-start.11 = (bf16[64,256]{1,0:T(8,128)(2,1)S(1)}, bf16[64,256]{1,0:T(8,128)(2,1)S(1)}, u32[]{:S(2)}, u32[]{:S(2)}) collective-permute-start(bf16[64,256]{1,0:T(8,128)(2,1)S(1)} %get-tuple-element.35), channel_id=1, source_target_pairs={{1,0},{2,1},{3,2},{4,3},{5,4},{6,5},{7,6},{8,7},{9,8},{10,9},{11,1... | collective-permute-start | bytes 98312 | tf_op jit(solution)/shard_map/ppermute | solution.py:24
  105.9 15.5 %collective-permute-start.12 = (bf16[64,256]{1,0:T(8,128)(2,1)S(1)}, bf16[64,256]{1,0:T(8,128)(2,1)S(1)}, u32[]{:S(2)}, u32[]{:S(2)}) collective-permute-start(bf16[64,256]{1,0:T(8,128)(2,1)S(1)} %get-tuple-element.37), channel_id=1, source_target_pairs={{0,1},{1,2},{2,3},{3,4},{4,5},{5,6},{6,7},{7,8},{8,9},{9,10},{10,1... | collective-permute-start | bytes 98312 | tf_op jit(solution)/shard_map/ppermute | solution.py:22
  111.7 9.7 %collective-permute-start.13 = (bf16[64,256]{1,0:T(8,128)(2,1)S(1)}, bf16[64,256]{1,0:T(8,128)(2,1)S(1)}, u32[]{:S(2)}, u32[]{:S(2)}) collective-permute-start(bf16[64,256]{1,0:T(8,128)(2,1)S(1)} %get-tuple-element.37), channel_id=1, source_target_pairs={{1,0},{2,1},{3,2},{4,3},{5,4},{6,5},{7,6},{8,7},{9,8},{10,9},{11,1... | collective-permute-start | bytes 98312 | tf_op jit(solution)/shard_map/ppermute | solution.py:24
  114.3 17.0 %collective-permute-start = (bf16[256,256]{0,1:T(8,128)(2,1)}, bf16[256,256]{0,1:T(8,128)(2,1)}, u32[]{:S(2)}, u32[]{:S(2)}) collective-permute-start(bf16[256,256]{0,1:T(8,128)(2,1)} %get-tuple-element.15), channel_id=1, source_target_pairs={{1,0},{2,1},{3,2},{4,3},{5,4},{6,5},{7,6},{8,7},{9,8},{10,9},{11,1... | collective-permute-start | bytes 393224 | tf_op jit(solution)/shard_map/ppermute | solution.py:11
  116.3 15.1 %collective-permute-start.1 = (bf16[256,256]{0,1:T(8,128)(2,1)}, bf16[256,256]{0,1:T(8,128)(2,1)}, u32[]{:S(2)}, u32[]{:S(2)}) collective-permute-start(bf16[256,256]{0,1:T(8,128)(2,1)} %get-tuple-element.16), channel_id=1, source_target_pairs={{0,1},{1,2},{2,3},{3,4},{4,5},{5,6},{6,7},{7,8},{8,9},{9,10},{10,1... | collective-permute-start | bytes 393224 | tf_op jit(solution)/shard_map/ppermute | solution.py:11
  130.0 144.2 %all-reduce.3.cloned.1.call-start = ((), (), s32[]{:S(2)}) async-start(), calls=%async_computation.1 | async-start | bytes 524288 | tf_op jit(solution)/shard_map/psum | solution.py:107
  133.1 813.1 %all-reduce.5.cloned.1.call-start = ((), (), s32[]{:S(2)}) async-start(), calls=%async_computation.2 | async-start | bytes 3538944 | tf_op jit(solution)/shard_map/psum | solution.py:134
  275.4 30.5 %copy-start.8 = (f32[64,256]{1,0:T(8,128)}, f32[64,256]{1,0:T(8,128)S(1)}, u32[]{:S(2)}) copy-start(f32[64,256]{1,0:T(8,128)S(1)} %get-tuple-element.40) | copy-start | bytes 196612
  276.8 28.1 %copy-start.7 = (bf16[64,64,9]{1,0,2:T(8,128)(2,1)S(1)}, bf16[64,64,9]{1,0,2:T(8,128)(2,1)}, u32[]{:S(2)}) copy-start(bf16[64,64,9]{1,0,2:T(8,128)(2,1)} %get-tuple-element.14) | copy-start | bytes 221188
  293.1 12.1 %collective-permute-start.14 = (bf16[64,256]{1,0:T(8,128)(2,1)S(1)}, bf16[64,256]{1,0:T(8,128)(2,1)S(1)}, u32[]{:S(2)}, u32[]{:S(2)}) collective-permute-start(bf16[64,256]{1,0:T(8,128)(2,1)S(1)} %get-tuple-element.27), channel_id=1, source_target_pairs={{1,0},{2,1},{3,2},{4,3},{5,4},{6,5},{7,6},{8,7},{9,8},{10,9},{11,1... | collective-permute-start | bytes 98312 | tf_op jit(solution)/shard_map/ppermute | solution.py:11
  300.6 5.3 collective-permute-start.15
  324.0 9.1 collective-permute-start.16
  325.9 7.2 collective-permute-start.17
  350.7 7.6 collective-permute-start.18
  352.6 6.3 collective-permute-start.19
  377.0 8.9 collective-permute-start.20
  378.9 7.0 collective-permute-start.21
  404.0 7.6 collective-permute-start.22
  406.0 6.4 collective-permute-start.23
  434.5 7.7 collective-permute-start.24
  436.4 6.7 collective-permute-start.25
  (38 other events, 236.3 us)
Sparse Core Ops, SparseCore 0:
  130.2 51.6 reduce-scatter.3
  185.6 88.6 all-reduce.2
  417.3 528.8 all-reduce.4
where the time goes:
time: 966 us; the launch traced here: 956 us
  waiting for transfers between devices  636 us (66%)
  other arithmetic  129 us (13%)
  starting transfers between devices  91.8 us (10%)
  local copies, waits for them, and re-layouts  47.1 us (5%)
  blocking collectives  21.8 us (2%)
  between operations  15.5 us (2%)
  matrix products  14.2 us (1%)
    psum x1, waiting for transfers between devices, per_device(): summed_weights = lax.psum(jnp.stack(layer_grads), 'sky') * normalizer  502 us
    scatter-add x7, other arithmetic, spread_columns(): return target.at[:, position.reshape(-1)].add(contrib.reshape(channels, -1))  110 us
    psum x1, waiting for transfers between devices, per_device(): summed = lax.psum(fold_unit_rims(unit_pad, row_count), 'branch')  69.8 us
    ppermute x14, starting transfers between devices, from_behind(): return lax.ppermute(value, axis, pairs)  56.7 us
    reduce_scatter x1, waiting for transfers between devices, per_device(): lax.psum_scatter(partial_sum.astype(jnp.bfloat16), 'branch', scatter_dime...  48.7 us
    gather x6, local copies, waits for them, and re-layouts, pick_columns(): jnp.take(padded, position.reshape(-1), axis=1).reshape(channels, 9, -1)  28 us
    all_gather x1, blocking collectives, per_device(): all_slopes = lax.all_gather(slope_share, 'branch', axis=0, tiled=True)  21.8 us
    ppermute x6, starting transfers between devices, with_halo(): lax.ppermute(tail, axis, [(i, (i + 1) % count) for i in range(ends)])  20.3 us
  transfers between devices with their start and end apart: 29, of which 11 were waited for; matrix products, arithmetic and copies ran while one was open for 6% of the time, Pallas kernels for 0%

commit v1 on v0

--- a/solution.py
+++ b/solution.py
@@ -104,7 +104,12 @@
         preferred_element_type=jnp.float32,
     )
     unit_pad = spread_columns(dec_terms, position, present, full_width, 3 * row_count)
-    summed = lax.psum(fold_unit_rims(unit_pad, row_count), "branch")
+
+    def obtain_the_core(x_part, axis_key):
+        current_value = lax.all_gather(x_part, axis_name=axis_key).sum(axis=0)
+        return current_value
+
+    summed = obtain_the_core(fold_unit_rims(unit_pad, row_count), "branch")
     all_slopes = lax.all_gather(slope_share, "branch", axis=0, tiled=True)
     unit_grad = (summed * all_slopes.astype(jnp.float32)).astype(jnp.bfloat16)
     gradient = lax.dot_general(

time: 966 us -> 923 us (0.955)
  waiting for transfers between devices: 636 us -> 596 us
    psum x1 -> x0, waiting for transfers between devices: 69.8 us -> none  [per_device(): summed = lax.psum(fold_unit_rims(unit_pad, row_count), 'branch')]
    all_gather x0 -> x1, waiting for transfers between devices: none -> 28.4 us  [obtain_the_core(): current_value = lax.all_gather(x_part, axis_name=axis_key).sum(axis=0)]
  transfers between devices with their start and end apart: 29 -> 29, of which waited for: 11 -> 13; matrix products, arithmetic and copies ran while one was open for 6% -> 6% of each run, Pallas kernels for 0% -> 0%
where the time goes in v1:
time: 923 us; the launch traced here: 914 us
  waiting for transfers between devices  596 us (65%)
  other arithmetic  128 us (14%)
  starting transfers between devices  92.4 us (10%)
  local copies, waits for them, and re-layouts  47.4 us (5%)
  blocking collectives  21.8 us (2%)
  between operations  15.4 us (2%)
  matrix products  12.3 us (1%)
    psum x1, waiting for transfers between devices, per_device(): summed_weights = lax.psum(jnp.stack(layer_grads), 'sky') * normalizer  503 us
    scatter-add x7, other arithmetic, spread_columns(): return target.at[:, position.reshape(-1)].add(contrib.reshape(channels, -1))  110 us
    ppermute x14, starting transfers between devices, from_behind(): return lax.ppermute(value, axis, pairs)  57.3 us
    reduce_scatter x1, waiting for transfers between devices, per_device(): lax.psum_scatter(partial_sum.astype(jnp.bfloat16), 'branch', scatter_dime...  48.7 us
    all_gather x1, waiting for transfers between devices, obtain_the_core(): current_value = lax.all_gather(x_part, axis_name=axis_key).sum(axis=0)  28.4 us
    gather x6, local copies, waits for them, and re-layouts, pick_columns(): jnp.take(padded, position.reshape(-1), axis=1).reshape(channels, 9, -1)  28 us
    all_gather x1, blocking collectives, per_device(): all_slopes = lax.all_gather(slope_share, 'branch', axis=0, tiled=True)  21.8 us
    ppermute x6, starting transfers between devices, with_halo(): lax.ppermute(tail, axis, [(i, (i + 1) % count) for i in range(ends)])  20.3 us
  transfers between devices with their start and end apart: 29, of which 13 were waited for; matrix products, arithmetic and copies ran while one was open for 6% of the time, Pallas kernels for 0%

profile of v1, /device:TPU:1, one launch (start us, length us, event | category | flops | bytes accessed | tf_op | source)
XLA Modules:
  0.0 913.7 jit_solution(11667547817191933423)
XLA Ops:
  7.2 6.2 collective-permute-start.2
  13.4 3.9 collective-permute-start.3
  21.3 4.7 gather_fusion
  34.3 3.1 collective-permute-done.5
  37.6 4.7 gather_fusion.1
  50.8 2.9 collective-permute-done.7
  53.8 4.7 gather_fusion.2
  65.2 5.2 collective-permute-done.9
  70.6 4.7 gather_fusion.3
  82.0 14.1 %scatter_custom_fusion = f32[256,768]{0,1:T(8,128)S(1)} fusion(s32[2304]{0:T(1024)S(1)} %fusion.94, f32[2304,256]{1,0:T(8,128)} %bitcast.225, f32[]{:T(128)} %constant.17.clone.1), kind=kCustom, calls=%fused_computation.81 | custom fusion | flops 589824 | bytes 786944 | tf_op jit(solution)/shard_map/scatter-add | solution.py:49
  97.0 4.7 gather_fusion.4
  105.0 5.8 collective-permute-start.12
  115.3 5.1 collective-permute-start.1
  120.7 4.7 gather_fusion.5
  132.2 48.7 %reduce-scatter.4.cloned.1.call-done = bf16[32,256]{1,0:T(8,128)(2,1)} async-done(((bf16[256,256]{1,0:T(8,128)(2,1)}), bf16[32,256]{1,0:T(8,128)(2,1)}) %reduce-scatter.4.cloned.1.call-update) | async-done | bytes 16400 | tf_op jit(solution)/shard_map/reduce_scatter | solution.py:95
  181.6 21.8 %all_gather.11 = bf16[256,256]{1,0:T(8,128)(2,1)S(1)} all-gather(bf16[32,256]{1,0:T(8,128)(2,1)S(1)} %fusion.83), channel_id=1, replica_groups=mesh['branch'=8,'sky'=64] {'branch'}, dimensions={0}, use_global_device_ids=true | all-gather | bytes 147456 | tf_op jit(solution)/shard_map/all_gather | solution.py:113
  203.6 28.4 %all-gather.3.cloned.1.call-done = f32[2048,256]{0,1:T(8,128)} async-done(((f32[256,256]{0,1:T(8,128)}), f32[2048,256]{0,1:T(8,128)}) %all-gather.3.cloned.1.call-update) | async-done | bytes 2097168 | tf_op jit(solution)/shard_map/all_gather | solution.py:109
  236.7 15.9 %scatter_custom_fusion.1 = f32[64,768]{0,1:T(8,128)S(1)} fusion(s32[2304]{0:T(1024)S(1)} %fusion.94, f32[64,2304]{0,1:T(8,128)S(1)} %copy.173, f32[]{:T(128)} %constant.17.clone.1, pred[2304]{0:T(1024)(128)(4,1)S(1)} %broadcast_in_dim.154), kind=kCustom, calls=%fused_computation.32 | custom fusion | flops 294912 | bytes 1380352 | tf_op jit(solution)/shard_map/scatter-add | solution.py:49
  252.8 8.0 collective-permute-start.14
  260.8 3.6 collective-permute-start.15
  267.0 15.9 %scatter_custom_fusion.2 = f32[64,768]{0,1:T(8,128)S(1)} fusion(s32[2304]{0:T(1024)S(1)} %fusion.94, f32[64,2304]{0,1:T(8,128)S(1)} %copy.177, f32[]{:T(128)} %constant.17.clone.1, pred[2304]{0:T(1024)(128)(4,1)S(1)} %broadcast_in_dim.154), kind=kCustom, calls=%fused_computation.30 | custom fusion | flops 294912 | bytes 1380352 | tf_op jit(solution)/shard_map/scatter-add | solution.py:49
  285.1 5.7 collective-permute-start.17
  293.1 16.2 %scatter_custom_fusion.3 = f32[64,768]{0,1:T(8,128)S(1)} fusion(s32[2304]{0:T(1024)} %copy-done.41, f32[64,2304]{0,1:T(8,128)S(1)} %copy.181, f32[]{:T(128)} %constant.17.clone.1, pred[2304]{0:T(1024)(128)(4,1)S(1)} %broadcast_in_dim.154), kind=kCustom, calls=%fused_computation.28 | custom fusion | flops 294912 | bytes 789760 | tf_op jit(solution)/shard_map/scatter-add | solution.py:49
  311.3 5.7 collective-permute-start.19
  319.9 16.2 %scatter_custom_fusion.4 = f32[64,768]{0,1:T(8,128)S(1)} fusion(s32[2304]{0:T(1024)} %copy-done.41, f32[64,2304]{0,1:T(8,128)S(1)} %copy.185, f32[]{:T(128)} %constant.17.clone.1, pred[2304]{0:T(1024)(128)(4,1)S(1)} %broadcast_in_dim.154), kind=kCustom, calls=%fused_computation.26 | custom fusion | flops 294912 | bytes 789760 | tf_op jit(solution)/shard_map/scatter-add | solution.py:49
  338.2 5.9 collective-permute-start.21
  345.9 16.0 %scatter_custom_fusion.5 = f32[64,768]{0,1:T(8,128)S(1)} fusion(s32[2304]{0:T(1024)} %copy-done.41, f32[64,2304]{0,1:T(8,128)S(1)} %copy.189, f32[]{:T(128)} %constant.17.clone.1, pred[2304]{0:T(1024)(128)(4,1)S(1)} %broadcast_in_dim.154), kind=kCustom, calls=%fused_computation.24 | custom fusion | flops 294912 | bytes 789760 | tf_op jit(solution)/shard_map/scatter-add | solution.py:49
  364.0 5.9 collective-permute-start.23
  375.9 16.0 %scatter_custom_fusion.6 = f32[64,768]{0,1:T(8,128)S(1)} fusion(s32[2304]{0:T(1024)} %copy-done.41, f32[64,2304]{0,1:T(8,128)S(1)} %copy.193, f32[]{:T(128)} %constant.17.clone.1, pred[2304]{0:T(1024)(128)(4,1)S(1)} %broadcast_in_dim.154), kind=kCustom, calls=%fused_computation.22 | custom fusion | flops 294912 | bytes 789760 | tf_op jit(solution)/shard_map/scatter-add | solution.py:49
  394.1 5.7 collective-permute-start.25
  401.5 502.6 %all-reduce.2.cloned.1.call-done = f32[6,9,64,64]{3,2,1,0:T(8,128)} async-done(((f32[6,9,64,64]{3,2,1,0:T(8,128)}), f32[6,9,64,64]{3,2,1,0:T(8,128)}) %all-reduce.2.cloned.1.call-update) | async-done | bytes 884752 | tf_op jit(solution)/shard_map/psum | solution.py:139
  904.1 2.9 multiply_bitcast_fusion
  (244 shorter events, 82.8 us)
Async XLA Ops:
  7.2 120.9 %copy-start = (bf16[256,64]{0,1:T(8,128)(2,1)S(1)}, bf16[256,64]{0,1:T(8,128)(2,1)}, u32[]{:S(2)}) copy-start(bf16[256,64]{0,1:T(8,128)(2,1)} %param.13) | copy-start | bytes 98308
  7.2 173.7 %reduce-scatter.4.cloned.1.call-start = ((), (), s32[]{:S(2)}) async-start(), calls=%async_computation.3 | async-start | bytes 147456 | tf_op jit(solution)/shard_map/reduce_scatter | solution.py:95
  7.2 12.3 %collective-permute-start.2 = (bf16[64,256]{1,0:T(8,128)(2,1)}, bf16[64,256]{1,0:T(8,128)(2,1)S(1)}, u32[]{:S(2)}, u32[]{:S(2)}) collective-permute-start(bf16[64,256]{1,0:T(8,128)(2,1)} %bitcast.247), channel_id=1, source_target_pairs={{0,1},{1,2},{2,3},{3,4},{4,5},{5,6},{6,7},{7,8},{8,9},{9,10},{10,1... | collective-permute-start | bytes 98312 | tf_op jit(solution)/shard_map/ppermute | solution.py:22
  13.4 7.0 collective-permute-start.3
  28.4 5.9 collective-permute-start.4
  30.7 6.7 collective-permute-start.5
  44.6 6.1 collective-permute-start.6
  46.6 7.1 collective-permute-start.7
  60.8 4.4 collective-permute-start.8
  63.0 7.4 collective-permute-start.9
  77.6 19.3 %collective-permute-start.10 = (bf16[64,256]{1,0:T(8,128)(2,1)S(1)}, bf16[64,256]{1,0:T(8,128)(2,1)S(1)}, u32[]{:S(2)}, u32[]{:S(2)}) collective-permute-start(bf16[64,256]{1,0:T(8,128)(2,1)S(1)} %get-tuple-element.35), channel_id=1, source_target_pairs={{0,1},{1,2},{2,3},{3,4},{4,5},{5,6},{6,7},{7,8},{8,9},{9,10},{10,1... | collective-permute-start | bytes 98312 | tf_op jit(solution)/shard_map/ppermute | solution.py:22
  79.5 17.3 %collective-permute-start.11 = (bf16[64,256]{1,0:T(8,128)(2,1)S(1)}, bf16[64,256]{1,0:T(8,128)(2,1)S(1)}, u32[]{:S(2)}, u32[]{:S(2)}) collective-permute-start(bf16[64,256]{1,0:T(8,128)(2,1)S(1)} %get-tuple-element.35), channel_id=1, source_target_pairs={{1,0},{2,1},{3,2},{4,3},{5,4},{6,5},{7,6},{8,7},{9,8},{10,9},{11,1... | collective-permute-start | bytes 98312 | tf_op jit(solution)/shard_map/ppermute | solution.py:24
  82.0 185.0 %copy-start.41 = (s32[2304]{0:T(1024)}, s32[2304]{0:T(1024)S(1)}, u32[]{:S(2)}) copy-start(s32[2304]{0:T(1024)S(1)} %fusion.94) | copy-start | bytes 27652
  105.0 15.5 %collective-permute-start.12 = (bf16[64,256]{1,0:T(8,128)(2,1)S(1)}, bf16[64,256]{1,0:T(8,128)(2,1)S(1)}, u32[]{:S(2)}, u32[]{:S(2)}) collective-permute-start(bf16[64,256]{1,0:T(8,128)(2,1)S(1)} %get-tuple-element.37), channel_id=1, source_target_pairs={{0,1},{1,2},{2,3},{3,4},{4,5},{5,6},{6,7},{7,8},{8,9},{9,10},{10,1... | collective-permute-start | bytes 98312 | tf_op jit(solution)/shard_map/ppermute | solution.py:22
  110.8 9.7 %collective-permute-start.13 = (bf16[64,256]{1,0:T(8,128)(2,1)S(1)}, bf16[64,256]{1,0:T(8,128)(2,1)S(1)}, u32[]{:S(2)}, u32[]{:S(2)}) collective-permute-start(bf16[64,256]{1,0:T(8,128)(2,1)S(1)} %get-tuple-element.37), channel_id=1, source_target_pairs={{1,0},{2,1},{3,2},{4,3},{5,4},{6,5},{7,6},{8,7},{9,8},{10,9},{11,1... | collective-permute-start | bytes 98312 | tf_op jit(solution)/shard_map/ppermute | solution.py:24
  113.4 15.7 %collective-permute-start = (bf16[256,256]{0,1:T(8,128)(2,1)}, bf16[256,256]{0,1:T(8,128)(2,1)}, u32[]{:S(2)}, u32[]{:S(2)}) collective-permute-start(bf16[256,256]{0,1:T(8,128)(2,1)} %get-tuple-element.15), channel_id=1, source_target_pairs={{1,0},{2,1},{3,2},{4,3},{5,4},{6,5},{7,6},{8,7},{9,8},{10,9},{11,1... | collective-permute-start | bytes 393224 | tf_op jit(solution)/shard_map/ppermute | solution.py:11
  115.3 13.8 %collective-permute-start.1 = (bf16[256,256]{0,1:T(8,128)(2,1)}, bf16[256,256]{0,1:T(8,128)(2,1)}, u32[]{:S(2)}, u32[]{:S(2)}) collective-permute-start(bf16[256,256]{0,1:T(8,128)(2,1)} %get-tuple-element.16), channel_id=1, source_target_pairs={{0,1},{1,2},{2,3},{3,4},{4,5},{5,6},{6,7},{7,8},{8,9},{9,10},{10,1... | collective-permute-start | bytes 393224 | tf_op jit(solution)/shard_map/ppermute | solution.py:11
  129.1 102.9 %all-gather.3.cloned.1.call-start = ((), (), s32[]{:S(2)}) async-start(), calls=%async_computation.2 | async-start | bytes 2359296 | tf_op jit(solution)/shard_map/all_gather | solution.py:109
  130.9 773.1 %all-reduce.2.cloned.1.call-start = ((), (), s32[]{:S(2)}) async-start(), calls=%async_computation.1 | async-start | bytes 3538944 | tf_op jit(solution)/shard_map/psum | solution.py:139
  235.5 29.7 %copy-start.9 = (f32[64,256]{1,0:T(8,128)}, f32[64,256]{1,0:T(8,128)S(1)}, u32[]{:S(2)}) copy-start(f32[64,256]{1,0:T(8,128)S(1)} %get-tuple-element.40) | copy-start | bytes 196612
  252.8 12.0 %collective-permute-start.14 = (bf16[64,256]{1,0:T(8,128)(2,1)S(1)}, bf16[64,256]{1,0:T(8,128)(2,1)S(1)}, u32[]{:S(2)}, u32[]{:S(2)}) collective-permute-start(bf16[64,256]{1,0:T(8,128)(2,1)S(1)} %get-tuple-element.27), channel_id=1, source_target_pairs={{1,0},{2,1},{3,2},{4,3},{5,4},{6,5},{7,6},{8,7},{9,8},{10,9},{11,1... | collective-permute-start | bytes 98312 | tf_op jit(solution)/shard_map/ppermute | solution.py:11
  260.8 4.4 collective-permute-start.15
  283.2 8.0 collective-permute-start.16
  285.1 6.7 collective-permute-start.17
  309.4 8.0 collective-permute-start.18
  311.3 6.7 collective-permute-start.19
  336.3 8.2 collective-permute-start.20
  338.2 6.8 collective-permute-start.21
  362.1 7.8 collective-permute-start.22
  364.0 6.9 collective-permute-start.23
  392.2 7.7 collective-permute-start.24
  394.1 6.7 collective-permute-start.25
  (39 other events, 278.6 us)
Sparse Core Ops, SparseCore 0:
  129.2 51.6 reduce-scatter.3
  183.8 48.1 all-gather.2
  374.9 529.0 all-reduce.1
